TPU v7x, 32 devices: a whole 2x2x4 slice. The times are simulated.
32 devices in a mesh: groups: 2 (over x), ep: 16 (over z, y, core).
Axes of the slice: x: 2, y: 2, z: 4, core: 2. Of those that a mesh axis runs over, the one named last changes fastest.
Arguments:
- resid: bfloat16 [4096, 2048], P(('groups', 'ep')), parts along dimension 0, may hold values from -12 to 12
- norm_gain: float32 [2048], replicated, may hold values from 0.1 to 1.9
- expert_ids: int32 [4096, 8], P(('groups', 'ep')), parts along dimension 0, may hold values from 0 to 15, as said below
- route_weights: float32 [4096, 8], P(('groups', 'ep')), parts along dimension 0, may hold values from 0.05 to 1
- w_in: bfloat16 [16, 2048, 1536], P('ep'), may hold values from -0.125 to 0.125
- w_out: bfloat16 [16, 768, 2048], P('ep'), may hold values from -0.21875 to 0.21875
Outputs:
- layer_out: bfloat16 [4096, 2048], P(('groups', 'ep')), parts along dimension 0
There are 2 independent parts, one for each index of `groups`. A program takes and returns all parts, laid end to end along the dimension named above; an argument that names none is the same for every part. Nothing has to cross between parts.
Inputs may be any that keep to these rules, and one draw needn't show every extreme that they name: `expert_ids`: each row names 8 different experts. Among the rows of one device no expert is named by more than 96 rows, and in every draw one expert is named by exactly 96 rows of every device.
All inputs are finite; a program needn't handle non-finite values.
Results may differ from a plain program's by a relative error of at most 0.0053.
Values may be sent and summed in bfloat16 or wider, within the bound.
A program may use at most 128 MiB of HBM per device.

v0:
```python
import jax
import jax.numpy as jnp
from jax import lax
from jax.sharding import PartitionSpec as P


def local(resid, norm_gain, expert_ids, route_weights, w_in, w_out):
    token_rows, model_width = resid.shape
    top_count = expert_ids.shape[1]
    ep_devices = lax.axis_size("ep")
    capacity = 3 * token_rows * top_count // (2 * ep_devices)
    weight_in = w_in[0]
    weight_out = w_out[0]
    hidden_units = weight_out.shape[0]
    resid_wide = resid.astype(jnp.float32)
    scale = lax.rsqrt(jnp.mean(resid_wide * resid_wide, axis=-1, keepdims=True) + 1e-06)
    normed = (resid_wide * scale * norm_gain).astype(jnp.bfloat16)
    mix_weights = route_weights / jnp.sum(route_weights, axis=-1, keepdims=True)
    flat_ids = expert_ids.reshape(-1)
    onehot = (flat_ids[:, None] == jnp.arange(ep_devices, dtype=jnp.int32)[None, :]).astype(
        jnp.int32
    )
    position = jnp.sum((jnp.cumsum(onehot, axis=0) - onehot) * onehot, axis=1)
    slot_index = flat_ids * capacity + position
    all_normed, all_ids = (
        lax.all_gather(normed, "ep", axis=0, tiled=True),
        lax.all_gather(expert_ids, "ep", axis=0, tiled=True),
    )
    own_expert = lax.axis_index("ep")
    row_hits = (
        jnp.any(all_ids == own_expert, axis=1).astype(jnp.int32).reshape(ep_devices, token_rows)
    )
    placing = jnp.cumsum(row_hits, axis=1) - row_hits
    target = jnp.where(
        row_hits == 1,
        jnp.arange(ep_devices, dtype=jnp.int32)[:, None] * capacity + placing,
        ep_devices * capacity,
    ).reshape(-1)
    received = (
        jnp.zeros((ep_devices * capacity, model_width), jnp.bfloat16)
        .at[target]
        .set(all_normed, mode="drop")
    )
    block_rows = received.reshape(ep_devices, capacity, model_width)
    rows_flat = block_rows.reshape(-1, model_width)
    projected = jnp.dot(rows_flat, weight_in, preferred_element_type=jnp.float32)
    activated = (jax.nn.silu(projected[:, :hidden_units]) * projected[:, hidden_units:]).astype(
        jnp.bfloat16
    )
    produced = jnp.dot(activated, weight_out, preferred_element_type=jnp.float32).astype(
        jnp.bfloat16
    )
    outputs = produced.reshape(block_rows.shape)
    returned = lax.all_to_all(outputs, "ep", split_axis=0, concat_axis=0, tiled=True).reshape(
        -1, model_width
    )
    picked = returned[slot_index].reshape(token_rows, top_count, model_width).astype(jnp.float32)
    mixed = jnp.sum(mix_weights[:, :, None] * picked, axis=1)
    return (resid_wide + mixed).astype(jnp.bfloat16)


def solution(mesh):
    in_specs = (
        P(("groups", "ep"), None),
        P(),
        P(("groups", "ep"), None),
        P(("groups", "ep"), None),
        P("ep", None, None),
        P("ep", None, None),
    )
    out_specs = P(("groups", "ep"), None)
    return jax.shard_map(local, mesh=mesh, in_specs=in_specs, out_specs=out_specs, check_vma=False)
```

profile of v0, /device:TPU:13, one launch (start us, length us, event | category | flops | bytes accessed | tf_op | source)
XLA Modules:
  0.0 294.2 jit_solution(109248182283365141)
XLA Ops:
  6.5 0.0 copy-start
  6.5 0.0 all-gather.2.cloned.1.call-start
  6.5 1.4 fusion.9
  7.9 2.0 fusion.11
  10.0 0.0 all-gather.2.cloned.1.call-update
  10.0 16.3 %all_gather.6 = s32[2048,8]{0,1:T(8,128)S(1)} all-gather(s32[128,8]{0,1:T(8,128)} %param.8), channel_id=1, replica_groups=mesh['groups'=2,'ep'=16] {'ep'}, dimensions={0}, use_global_device_ids=true | all-gather | bytes 69632 | tf_op jit(solution)/shard_map/all_gather | solution.py:27
  26.4 0.3 reduce_window_sum.28
  26.6 0.1 add.70
  26.7 58.2 %all-gather.2.cloned.1.call-done = bf16[2048,2048]{1,0:T(8,128)(2,1)} async-done(((bf16[128,2048]{1,0:T(8,128)(2,1)}), bf16[2048,2048]{1,0:T(8,128)(2,1)}) %all-gather.2.cloned.1.call-update) | async-done | bytes 8388624 | tf_op jit(solution)/shard_map/all_gather | solution.py:26
  84.9 16.9 %scatter_custom_fusion = bf16[1536,2048]{1,0:T(8,128)(2,1)} fusion(s32[2048]{0:T(1024)S(1)} %bitcast.46, bf16[2048,2048]{1,0:T(8,128)(2,1)} %all-gather.2.cloned.1.call-done, bf16[]{:T(256)} %constant.12.clone.1), kind=kCustom, calls=%fused_computation.10 | custom fusion | bytes 6291968 | tf_op jit(solution)/shard_map/scatter | solution.py:42
  101.8 14.1 %fusion.1 = f32[1536,1536]{1,0:T(8,128)S(1)} fusion(bf16[1536,2048]{1,0:T(8,128)(2,1)} %scatter_custom_fusion, bf16[1,2048,1536]{2,1,0:T(8,128)(2,1)} %param.10), kind=kOutput, calls=%fused_computation.5 | convolution fusion | flops 9663676416 | bytes 22020096 | tf_op jit(solution)/shard_map/dot_general | solution.py:46
  115.9 0.0 copy-done
  115.9 7.0 %convolution_convert_fusion = bf16[1536,2048]{1,0:T(8,128)(2,1)} fusion(bf16[1,768,2048]{2,1,0:T(8,128)(2,1)S(1)} %copy-done, f32[1536,1536]{1,0:T(8,128)S(1)} %fusion.1), kind=kOutput, calls=%fused_computation.4 | convolution fusion | flops 4842061824 | bytes 18874368 | tf_op jit(solution)/shard_map/dot_general | solution.py:50
  122.9 0.0 copy-start.1
  122.9 0.0 copy-start.2
  122.9 6.1 %all-to-all-start = ((bf16[16,96,2048]{2,1,0:T(8,128)(2,1)}), bf16[16,96,2048]{2,1,0:T(8,128)(2,1)}, u32[]{:S(2)}, u32[]{:S(2)}) async-start(bf16[16,96,2048]{2,1,0:T(8,128)(2,1)} %bitcast.38), calls=%async_computation | async-start | bytes 12582912 | tf_op jit(solution)/shard_map/all_to_all | solution.py:54
  129.0 0.0 copy-done.1
  129.0 0.1 copy.12
  129.1 0.1 eq.53
  129.2 0.1 eq.49
  129.3 0.1 copy.11
  129.4 0.1 mul.72
  129.6 4.5 %reduce-window.6 = s32[16,8,128]{2,1,0:T(8,128)S(1)} reduce-window(s32[16,8,128]{2,1,0:T(8,128)S(1)} %fusion.16, s32[]{:T(128)} %constant.8.clone.1), window={size=1x1x128 pad=0_0x0_0x127_0}, to_apply=%region_5.6 | reduce-window | flops 2080768 | bytes 131076 | tf_op jit(solution)/shard_map/reduce-window
  134.1 0.1 slice.20
  134.2 0.1 copy.14
  134.3 0.1 copy.15
  134.4 0.0 copy-done.2
  134.4 0.1 copy.10
  134.5 0.1 broadcast_add_fusion
  134.7 131.8 %all-to-all-done = bf16[16,96,2048]{2,1,0:T(8,128)(2,1)} async-done(((bf16[16,96,2048]{2,1,0:T(8,128)(2,1)}), bf16[16,96,2048]{2,1,0:T(8,128)(2,1)}, u32[]{:S(2)}, u32[]{:S(2)}) %all-to-all-start) | async-done | bytes 6291488 | tf_op jit(solution)/shard_map/all_to_all | solution.py:54
  266.5 12.4 %gather_fusion = bf16[1024,2048]{1,0:T(8,128)(2,1)} fusion(bf16[1536,2048]{1,0:T(8,128)(2,1)} %bitcast.8, s32[1024]{0:T(1024)S(1)} %broadcast_clamp_fusion), kind=kCustom, calls=%fused_computation | custom fusion | bytes 8392704 | tf_op jit(solution)/shard_map/gather | solution.py:57
  278.9 6.5 %fusion = f32[128,2048]{1,0:T(8,128)S(1)} fusion(bf16[1024,2048]{1,0:T(8,128)(2,1)} %gather_fusion, f32[128,8]{1,0:T(8,128)S(1)} %copy.10), kind=kLoop, calls=%fused_computation.3 | loop fusion | flops 6029312 | bytes 5246976 | tf_op jit(solution)/shard_map/reduce_sum | solution.py:58
  285.4 2.0 fusion.12
  (14 shorter events, 0.2 us)
Async XLA Ops:
  6.5 109.4 %copy-start = (bf16[1,768,2048]{2,1,0:T(8,128)(2,1)S(1)}, bf16[1,768,2048]{2,1,0:T(8,128)(2,1)}, u32[]{:S(2)}) copy-start(bf16[1,768,2048]{2,1,0:T(8,128)(2,1)} %param.11) | copy-start | bytes 9437188
  6.5 78.4 %all-gather.2.cloned.1.call-start = ((), (), s32[]{:S(2)}) async-start(), calls=%async_computation.1 | async-start | bytes 8912896 | tf_op jit(solution)/shard_map/all_gather | solution.py:26
  122.9 6.1 %copy-start.1 = (s32[128,8]{0,1:T(8,128)S(1)}, s32[128,8]{0,1:T(8,128)}, u32[]{:S(2)}) copy-start(s32[128,8]{0,1:T(8,128)} %param.8) | copy-start | bytes 12292
  122.9 11.5 %copy-start.2 = (f32[128,8]{0,1:T(8,128)S(1)}, f32[128,8]{0,1:T(8,128)}, u32[]{:S(2)}) copy-start(f32[128,8]{0,1:T(8,128)} %param.9) | copy-start | bytes 12292
  122.9 143.5 %all-to-all-start = ((bf16[16,96,2048]{2,1,0:T(8,128)(2,1)}), bf16[16,96,2048]{2,1,0:T(8,128)(2,1)}, u32[]{:S(2)}, u32[]{:S(2)}) async-start(bf16[16,96,2048]{2,1,0:T(8,128)(2,1)} %bitcast.38), calls=%async_computation | async-start | bytes 12582912 | tf_op jit(solution)/shard_map/all_to_all | solution.py:54
Sparse Core Ops, SparseCore 0:
  10.1 74.7 all-gather.1
where the time goes:
time: 295 us; the launch traced here: 294 us
  waiting for transfers between devices  190 us (64%)
  local copies, waits for them, and re-layouts  30.2 us (10%)
  matrix products  21.1 us (7%)
  other arithmetic  17 us (6%)
  blocking collectives  16.3 us (6%)
  between operations  13.5 us (5%)
  starting transfers between devices  6.11 us (2%)
    all_to_all x1, waiting for transfers between devices, local(): lax.all_to_all(outputs, 'ep', split_axis=0, concat_axis=0, tiled=True)  132 us
    all_gather x1, waiting for transfers between devices, local(): lax.all_gather(normed, 'ep', axis=0, tiled=True)  58.2 us
    scatter x1, local copies, waits for them, and re-layouts, local(): received = jnp.zeros((ep_devices * capacity, model_width), jnp.bfloat16)....  16.9 us
    all_gather x1, blocking collectives, local(): lax.all_gather(expert_ids, 'ep', axis=0, tiled=True)  16.3 us
    dot_general x1, matrix products, local(): jnp.dot(rows_flat, weight_in, preferred_element_type=jnp.float32)  14.1 us
    gather x1, local copies, waits for them, and re-layouts, local(): returned[slot_index].reshape(token_rows, top_count, model_width)  12.4 us
    dot_general x1, matrix products, local(): jnp.dot(activated, weight_out, preferred_element_type=jnp.float32)  6.98 us
    reduce_sum x1, other arithmetic, local(): mixed = jnp.sum(mix_weights[:, :, None] * picked, axis=1)  6.52 us
  transfers between devices with their start and end apart: 2, of which 2 were waited for; matrix products, arithmetic and copies ran while one was open for 2% of the time, Pallas kernels for 0%

commit v1 on v0

--- a/solution.py
+++ b/solution.py
@@ -1,10 +1,284 @@
+import functools
+
 import jax
 import jax.numpy as jnp
 from jax import lax
+from jax.experimental import pallas as pl
+from jax.experimental.pallas import tpu as pltpu
 from jax.sharding import PartitionSpec as P
 
 
+PLANE = 4
+MESH = pl.DeviceIdType.MESH
+
+
+def flip(index, bits):
+    bit = 1
+    while bit <= bits:
+        if bits & bit:
+            index = index + bit - 2 * bit * ((index // bit) % 2)
+        bit *= 2
+    return index
+
+
+def moe_kernel(
+    count, x_ref, table_ref, resid_ref, win_hbm, wout_hbm, o_ref,
+    gathered, weights, weight_cols, win, wout, hidden, partial, from_core, from_y, from_z,
+    load_sem, table_send, table_recv, z_send, z_recv, y_send, y_recv, core_send, core_recv,
+    fwd_send, fwd_recv, rc_send, rc_recv, ry_send, ry_recv, rz_send, rz_recv,
+):
+    rows, width = x_ref.shape
+    units = wout.shape[0]
+    planes = count // PLANE
+    me = lax.axis_index("ep")
+    z, q = me // PLANE, me % PLANE
+    y, c = q // 2, q % 2
+    core_mate = z * PLANE + flip(q, 1)
+    y_mate = z * PLANE + flip(q, 2)
+
+    def remote(src, dst, send, recv, target):
+        return pltpu.make_async_remote_copy(
+            src_ref=src, dst_ref=dst, send_sem=send, recv_sem=recv,
+            device_id={"ep": target}, device_id_type=MESH,
+        )
+
+    load_in = pltpu.make_async_copy(win_hbm.at[0], win, load_sem.at[0])
+    load_out = pltpu.make_async_copy(wout_hbm.at[0], wout, load_sem.at[1])
+    load_in.start()
+    load_out.start()
+
+    barrier = pltpu.get_barrier_semaphore()
+    for k in range(1, count):
+        pl.semaphore_signal(
+            barrier, inc=1, device_id={"ep": lax.rem(me + k, count)}, device_id_type=MESH
+        )
+    pl.semaphore_wait(barrier, count - 1)
+
+    started = []
+
+    def begin(copy):
+        copy.start()
+        started.append(copy)
+        return copy
+
+    plane_of = [flip(z, s) for s in range(planes)]
+    to_z, to_y, to_core, to_fwd = {}, {}, {}, {}
+    red_core, red_y, red_z = {}, {}, {}
+
+    def spread(s):
+        src = x_ref if s == 0 else gathered.at[plane_of[s], q]
+        dst = gathered.at[plane_of[s], q]
+        to_y[s] = begin(remote(src, dst, y_send.at[s], y_recv.at[s], y_mate))
+        to_core[s] = begin(remote(src, dst, core_send.at[s], core_recv.at[s], core_mate))
+
+    def forward(s):
+        to_y[s].wait_recv()
+        block = gathered.at[plane_of[s], flip(q, 2)]
+        to_fwd[s] = begin(remote(block, block, fwd_send.at[s], fwd_recv.at[s], core_mate))
+
+    spread(0)
+    for s in range(1, planes):
+        to_z[s] = begin(
+            remote(
+                x_ref, gathered.at[z, q], z_send.at[s], z_recv.at[s],
+                plane_of[s] * PLANE + q,
+            )
+        )
+    tables = []
+    for k in range(1, count):
+        target = lax.rem(me + k, count)
+        tables.append(
+            begin(
+                remote(
+                    table_ref.at[target], weights.at[me],
+                    table_send.at[k - 1], table_recv.at[k - 1], target,
+                )
+            )
+        )
+    gathered[z, q] = x_ref[...]
+    weights[me] = table_ref[me]
+    for copy in tables:
+        copy.wait_recv()
+
+    tile_in = 256 if units % 256 == 0 else units
+    tile_out = 512 if width % 512 == 0 else width
+
+    def experts(s):
+        plane = plane_of[s]
+        eye = lax.broadcasted_iota(jnp.int32, (rows, rows), 0) == lax.broadcasted_iota(
+            jnp.int32, (rows, rows), 1
+        )
+        for k in range(PLANE):
+            lane = jnp.broadcast_to(weights[plane * PLANE + k], (rows, rows))
+            column = jnp.sum(jnp.where(eye, lane, 0.0), axis=1, keepdims=True)
+            weight_cols[pl.ds(k * rows, rows), :] = jnp.broadcast_to(column, (rows, 128))
+
+        @pl.loop(0, units // tile_in)
+        def _(j):
+            gate_at = pl.multiple_of(j * tile_in, 128)
+            up_at = pl.multiple_of(units + j * tile_in, 128)
+            block = gathered[plane].reshape(PLANE * rows, width)
+            gate = jnp.dot(
+                block, win[:, pl.ds(gate_at, tile_in)], preferred_element_type=jnp.float32
+            )
+            up = jnp.dot(block, win[:, pl.ds(up_at, tile_in)], preferred_element_type=jnp.float32)
+            act = gate / (1.0 + jnp.exp(-gate)) * up
+            hidden[:, pl.ds(gate_at, tile_in)] = act.astype(jnp.bfloat16)
+
+        @pl.loop(0, width // tile_out)
+        def _(j):
+            at = pl.multiple_of(j * tile_out, 128)
+            made = jnp.dot(
+                hidden[...], wout[:, pl.ds(at, tile_out)], preferred_element_type=jnp.float32
+            )
+            made = made.astype(jnp.bfloat16).astype(jnp.float32)
+            for k in range(PLANE):
+                cols = weight_cols[pl.ds(k * rows, rows), :]
+                pieces = [
+                    made[k * rows : (k + 1) * rows, i * 128 : (i + 1) * 128] * cols
+                    for i in range(tile_out // 128)
+                ]
+                partial[s, k % 2, k // 2, :, pl.ds(at, tile_out)] = jnp.concatenate(
+                    pieces, axis=1
+                ).astype(jnp.bfloat16)
+
+    def reduce_core(s):
+        red_core[s] = begin(
+            remote(
+                partial.at[s, flip(c, 1)], from_core.at[s], rc_send.at[s], rc_recv.at[s], core_mate
+            )
+        )
+
+    step = 16
+
+    def reduce_y(s):
+        red_core[s].wait_recv()
+
+        @pl.loop(0, rows // step)
+        def _(i):
+            at = pl.ds(pl.multiple_of(i * step, step), step)
+            for k in range(2):
+                total = partial[s, c, k, at, :].astype(jnp.float32) + from_core[
+                    s, k, at, :
+                ].astype(jnp.float32)
+                partial[s, c, k, at, :] = total.astype(jnp.bfloat16)
+
+        red_y[s] = begin(
+            remote(
+                partial.at[s, c, flip(y, 1)], from_y.at[s], ry_send.at[s], ry_recv.at[s], y_mate
+            )
+        )
+
+    def reduce_z(s):
+        red_y[s].wait_recv()
+
+        @pl.loop(0, rows // step)
+        def _(i):
+            at = pl.ds(pl.multiple_of(i * step, step), step)
+            total = partial[s, c, y, at, :].astype(jnp.float32) + from_y[s, at, :].astype(
+                jnp.float32
+            )
+            partial[s, c, y, at, :] = total.astype(jnp.bfloat16)
+
+        if s:
+            red_z[s] = begin(
+                remote(
+                    partial.at[s, c, y], from_z.at[s - 1], rz_send.at[s], rz_recv.at[s],
+                    plane_of[s] * PLANE + q,
+                )
+            )
+
+    def arrive(s):
+        if s < planes:
+            to_z[s].wait_recv()
+            spread(s)
+
+    forward(0)
+    arrive(1)
+    load_in.wait()
+    load_out.wait()
+    for s in range(planes):
+        to_core[s].wait_recv()
+        to_fwd[s].wait_recv()
+        experts(s)
+        reduce_core(s)
+        arrive(s + 2)
+        if s + 1 < planes:
+            forward(s + 1)
+        reduce_y(s)
+        if s:
+            reduce_z(s - 1)
+    reduce_z(planes - 1)
+    for s in range(1, planes):
+        red_z[s].wait_recv()
+
+    @pl.loop(0, rows // step)
+    def _(i):
+        at = pl.ds(pl.multiple_of(i * step, step), step)
+        total = partial[0, c, y, at, :].astype(jnp.float32)
+        for s in range(1, planes):
+            total = total + from_z[s - 1, at, :].astype(jnp.float32)
+        o_ref[at, :] = (resid_ref[at, :].astype(jnp.float32) + total).astype(jnp.bfloat16)
+
+    for copy in started:
+        copy.wait_send()
+
+
+def vmem_bytes(count, rows, width, units):
+    block = 2 * rows * width
+    return (
+        block * (4 * 2 * (count // PLANE) + 8) + 2 * 3 * units * width
+        + 2 * PLANE * rows * units + 8 * count * rows * 4
+    )
+
+
 def local(resid, norm_gain, expert_ids, route_weights, w_in, w_out):
+    rows, width = resid.shape
+    units = w_out.shape[1]
+    count = lax.axis_size("ep")
+    planes = count // PLANE
+    fits = vmem_bytes(count, rows, width, units) <= 44 * 2**20
+    if count % PLANE or planes < 2 or planes & (planes - 1) or rows != 128 or not fits:
+        return local_wide(resid, norm_gain, expert_ids, route_weights, w_in, w_out)
+    resid_wide = resid.astype(jnp.float32)
+    scale = lax.rsqrt(jnp.mean(resid_wide * resid_wide, axis=-1, keepdims=True) + 1e-06)
+    normed = (resid_wide * scale * norm_gain).astype(jnp.bfloat16)
+    mix_weights = route_weights / jnp.sum(route_weights, axis=-1, keepdims=True)
+    experts = jnp.arange(count, dtype=jnp.int32)[:, None, None]
+    table = jnp.sum(jnp.where(expert_ids[None] == experts, mix_weights[None], 0.0), axis=-1)
+    table = table.reshape(count, 1, rows)
+    vmem = pl.BlockSpec(memory_space=pltpu.VMEM)
+    hbm = pl.BlockSpec(memory_space=pl.ANY)
+    bf16 = jnp.bfloat16
+    dma = pltpu.SemaphoreType.DMA
+    return pl.pallas_call(
+        functools.partial(moe_kernel, count),
+        out_shape=jax.ShapeDtypeStruct((rows, width), bf16),
+        in_specs=[vmem, vmem, vmem, hbm, hbm],
+        out_specs=vmem,
+        scratch_shapes=[
+            pltpu.VMEM((planes, PLANE, rows, width), bf16),
+            pltpu.VMEM((count, 1, rows), jnp.float32),
+            pltpu.VMEM((PLANE * rows, 128), jnp.float32),
+            pltpu.VMEM((width, 2 * units), bf16),
+            pltpu.VMEM((units, width), bf16),
+            pltpu.VMEM((PLANE * rows, units), bf16),
+            pltpu.VMEM((planes, 2, 2, rows, width), bf16),
+            pltpu.VMEM((planes, 2, rows, width), bf16),
+            pltpu.VMEM((planes, rows, width), bf16),
+            pltpu.VMEM((planes - 1, rows, width), bf16),
+            dma((2,)),
+            dma((count - 1,)),
+            dma((count - 1,)),
+        ]
+        + [dma((planes,))] * 14,
+        compiler_params=pltpu.CompilerParams(
+            collective_id=0, has_side_effects=True, vmem_limit_bytes=60 * 2**20
+        ),
+    )(normed, table, resid, w_in, w_out)
+
+
+def local_wide(resid, norm_gain, expert_ids, route_weights, w_in, w_out):
     token_rows, model_width = resid.shape
     top_count = expert_ids.shape[1]
     ep_devices = lax.axis_size("ep")

time: 295 us -> 178 us (0.60)
  the two profiles are of different devices: /device:TPU:13 before, /device:TPU:10 now
where the time goes in v1:
time: 178 us
  Pallas kernels  170 us (96%)
  other arithmetic  5.96 us (3%)
  local copies, waits for them, and re-layouts  1.88 us (1%)
    pallas_call x1, Pallas kernels, local(): pl.pallas_call(functools.partial(moe_kernel, count), out_shape=jax.ShapeD...  170 us

profile of v1, /device:TPU:10, one launch (start us, length us, event | category | flops | bytes accessed | tf_op | source)
XLA Modules:
  0.0 177.5 jit_solution(14033419863007878680)
XLA Ops:
  0.0 0.7 reduce_sum.28
  0.7 1.2 fusion
  1.9 0.7 broadcast_divide_fusion
  2.6 1.3 select_reduce_fusion
  3.9 2.0 %fusion.2.x_ref = bf16[128,2048]{1,0:T(8,128)(2,1)} fusion(bf16[128,2048]{1,0:T(8,128)(2,1)} %resid_ref.1, f32[2048]{0:T(1024)} %param.7, f32[128]{0:T(128)S(1)} %add_rsqrt_fusion), kind=kLoop, calls=%fused_computation.4 | loop fusion | flops 1048576 | bytes 1057280 | tf_op jit(solution)/shard_map/convert_element_type | solution.py:245
  6.0 169.7 %shard_map.64 = bf16[128,2048]{1,0:T(8,128)(2,1)} custom-call(bf16[128,2048]{1,0:T(8,128)(2,1)} %fusion.2.x_ref, f32[16,1,128]{2,1,0:T(1,128)} %bitcast.1, bf16[128,2048]{1,0:T(8,128)(2,1)} %resid_ref.1, bf16[1,2048,1536]{2,1,0:T(8,128)(2,1)} %win_hbm.1, bf16[1,768,2048]{2,1,0:T(8,128)(2,1)} %wout_hbm.1), custom_call_target="tpu_custom_call" | custom-call | tf_op jit(solution)/shard_map/pallas_call | solution.py:254
  175.6 1.9 %copy.10 = bf16[128,2048]{1,0:T(8,128)(2,1)} copy(bf16[128,2048]{1,0:T(8,128)(2,1)} %shard_map.64) | data formatting | bytes 1048576
  (1 shorter events, 0.0 us)

commit v2 on v1

--- a/solution.py
+++ b/solution.py
@@ -61,13 +61,32 @@
         started.append(copy)
         return copy
 
-    plane_of = [flip(z, s) for s in range(planes)]
-    to_z, to_y, to_core, to_fwd = {}, {}, {}, {}
+    low, high = z, planes - 1 - z
+    near = jnp.minimum(low, high)
+    side = jnp.where(low < high, -1, 1)
+
+    def visit(k):
+        if k == 0:
+            return z
+        paired = (side if k % 2 else -side) * ((k + 1) // 2)
+        return z + jnp.where(k <= 2 * near, paired, -side * (k - near))
+
+    plane_of = [visit(k) for k in range(planes)]
+    to_y, to_core, to_fwd = {}, {}, {}
     red_core, red_y, red_z = {}, {}, {}
+    guarded = []
+
+    def begin_if(condition, copy):
+        @pl.when(condition)
+        def _():
+            copy.start()
+
+        guarded.append((condition, copy))
 
     def spread(s):
-        src = x_ref if s == 0 else gathered.at[plane_of[s], q]
-        dst = gathered.at[plane_of[s], q]
+        p = plane_of[s]
+        src = x_ref if s == 0 else gathered.at[p, q]
+        dst = gathered.at[p, q]
         to_y[s] = begin(remote(src, dst, y_send.at[s], y_recv.at[s], y_mate))
         to_core[s] = begin(remote(src, dst, core_send.at[s], core_recv.at[s], core_mate))
 
@@ -76,14 +95,14 @@
         block = gathered.at[plane_of[s], flip(q, 2)]
         to_fwd[s] = begin(remote(block, block, fwd_send.at[s], fwd_recv.at[s], core_mate))
 
+    def z_copy(p, src, send, target_plane):
+        return remote(
+            src, gathered.at[p, q], z_send.at[send], z_recv.at[p], target_plane * PLANE + q
+        )
+
     spread(0)
-    for s in range(1, planes):
-        to_z[s] = begin(
-            remote(
-                x_ref, gathered.at[z, q], z_send.at[s], z_recv.at[s],
-                plane_of[s] * PLANE + q,
-            )
-        )
+    begin_if(z > 0, z_copy(z, x_ref, 0, jnp.maximum(z - 1, 0)))
+    begin_if(z < planes - 1, z_copy(z, x_ref, planes, jnp.minimum(z + 1, planes - 1)))
     tables = []
     for k in range(1, count):
         target = lax.rem(me + k, count)
@@ -97,8 +116,17 @@
         )
     gathered[z, q] = x_ref[...]
     weights[me] = table_ref[me]
-    for copy in tables:
-        copy.wait_recv()
+
+    def arrive(s):
+        if s >= planes:
+            return
+        p = plane_of[s]
+        block = gathered.at[p, q]
+        z_copy(p, block, s, p).wait_recv()
+        onward = jnp.where(p < z, z + 1, z - 1)
+        inside = jnp.logical_and(onward >= 0, onward < planes)
+        begin_if(inside, z_copy(p, block, s, jnp.clip(onward, 0, planes - 1)))
+        spread(s)
 
     tile_in = 256 if units % 256 == 0 else units
     tile_out = 512 if width % 512 == 0 else width
@@ -183,20 +211,17 @@
         if s:
             red_z[s] = begin(
                 remote(
-                    partial.at[s, c, y], from_z.at[s - 1], rz_send.at[s], rz_recv.at[s],
+                    partial.at[s, c, y], from_z.at[z], rz_send.at[s], rz_recv.at[z],
                     plane_of[s] * PLANE + q,
                 )
             )
 
-    def arrive(s):
-        if s < planes:
-            to_z[s].wait_recv()
-            spread(s)
-
+    arrive(1)
     forward(0)
-    arrive(1)
     load_in.wait()
     load_out.wait()
+    for copy in tables:
+        copy.wait_recv()
     for s in range(planes):
         to_core[s].wait_recv()
         to_fwd[s].wait_recv()
@@ -205,23 +230,34 @@
         arrive(s + 2)
         if s + 1 < planes:
             forward(s + 1)
-        reduce_y(s)
         if s:
+            reduce_y(s)
+        if s > 1:
             reduce_z(s - 1)
+    reduce_y(0)
     reduce_z(planes - 1)
+    reduce_z(0)
     for s in range(1, planes):
-        red_z[s].wait_recv()
+        p = plane_of[s]
+        remote(
+            partial.at[0, c, y], from_z.at[p], rz_send.at[s], rz_recv.at[p], p * PLANE + q
+        ).wait_recv()
 
     @pl.loop(0, rows // step)
     def _(i):
         at = pl.ds(pl.multiple_of(i * step, step), step)
         total = partial[0, c, y, at, :].astype(jnp.float32)
         for s in range(1, planes):
-            total = total + from_z[s - 1, at, :].astype(jnp.float32)
+            total = total + from_z[plane_of[s], at, :].astype(jnp.float32)
         o_ref[at, :] = (resid_ref[at, :].astype(jnp.float32) + total).astype(jnp.bfloat16)
 
     for copy in started:
         copy.wait_send()
+    for condition, copy in guarded:
+
+        @pl.when(condition)
+        def _(copy=copy):
+            copy.wait_send()
 
 
 def vmem_bytes(count, rows, width, units):
@@ -266,12 +302,12 @@
             pltpu.VMEM((planes, 2, 2, rows, width), bf16),
             pltpu.VMEM((planes, 2, rows, width), bf16),
             pltpu.VMEM((planes, rows, width), bf16),
-            pltpu.VMEM((planes - 1, rows, width), bf16),
+            pltpu.VMEM((planes, rows, width), bf16),
             dma((2,)),
             dma((count - 1,)),
             dma((count - 1,)),
         ]
-        + [dma((planes,))] * 14,
+        + [dma((planes + 1,))] * 14,
         compiler_params=pltpu.CompilerParams(
             collective_id=0, has_side_effects=True, vmem_limit_bytes=60 * 2**20
         ),

time: 178 us -> 134 us (0.75)
  the two profiles are of different devices: /device:TPU:10 before, /device:TPU:0 now
where the time goes in v2:
time: 134 us; the launch traced here: 133 us
  Pallas kernels  126 us (94%)
  other arithmetic  5.96 us (4%)
  local copies, waits for them, and re-layouts  1.88 us (1%)
    pallas_call x1, Pallas kernels, local(): pl.pallas_call(functools.partial(moe_kernel, count), out_shape=jax.ShapeD...  126 us

profile of v2, /device:TPU:0, one launch (start us, length us, event | category | flops | bytes accessed | tf_op | source)
XLA Modules:
  0.0 133.4 jit_solution(2137574691143457830)
XLA Ops:
  0.0 0.7 reduce_sum.28
  0.7 1.2 fusion
  1.9 0.7 broadcast_divide_fusion
  2.6 1.3 select_reduce_fusion
  3.9 2.0 %fusion.2.x_ref = bf16[128,2048]{1,0:T(8,128)(2,1)} fusion(bf16[128,2048]{1,0:T(8,128)(2,1)} %resid_ref.1, f32[2048]{0:T(1024)} %param.7, f32[128]{0:T(128)S(1)} %add_rsqrt_fusion), kind=kLoop, calls=%fused_computation.4 | loop fusion | flops 1048576 | bytes 1057280 | tf_op jit(solution)/shard_map/convert_element_type | solution.py:281
  6.0 125.6 %shard_map.64 = bf16[128,2048]{1,0:T(8,128)(2,1)} custom-call(bf16[128,2048]{1,0:T(8,128)(2,1)} %fusion.2.x_ref, f32[16,1,128]{2,1,0:T(1,128)} %bitcast.1, bf16[128,2048]{1,0:T(8,128)(2,1)} %resid_ref.1, bf16[1,2048,1536]{2,1,0:T(8,128)(2,1)} %win_hbm.1, bf16[1,768,2048]{2,1,0:T(8,128)(2,1)} %wout_hbm.1), custom_call_target="tpu_custom_call" | custom-call | tf_op jit(solution)/shard_map/pallas_call | solution.py:290
  131.6 1.9 %copy.10 = bf16[128,2048]{1,0:T(8,128)(2,1)} copy(bf16[128,2048]{1,0:T(8,128)(2,1)} %shard_map.64) | data formatting | bytes 1048576
  (1 shorter events, 0.0 us)

commit v3 on v2

--- a/solution.py
+++ b/solution.py
@@ -22,12 +22,13 @@
 
 
 def moe_kernel(
-    count, x_ref, table_ref, resid_ref, win_hbm, wout_hbm, o_ref,
-    gathered, weights, weight_cols, win, wout, hidden, partial, from_core, from_y, from_z,
+    count, resid_ref, gain_ref, ids_ref, route_ref, win_hbm, wout_hbm, o_ref,
+    gathered, table_ref, weights, weight_cols, win, wout, hidden, partial, from_core, from_y,
+    from_z, from_near,
     load_sem, table_send, table_recv, z_send, z_recv, y_send, y_recv, core_send, core_recv,
-    fwd_send, fwd_recv, rc_send, rc_recv, ry_send, ry_recv, rz_send, rz_recv,
+    fwd_send, fwd_recv, rc_send, rc_recv, ry_send, ry_recv, rz_send, rz_recv, rn_send, rn_recv,
 ):
-    rows, width = x_ref.shape
+    rows, width = resid_ref.shape
     units = wout.shape[0]
     planes = count // PLANE
     me = lax.axis_index("ep")
@@ -52,6 +53,20 @@
         pl.semaphore_signal(
             barrier, inc=1, device_id={"ep": lax.rem(me + k, count)}, device_id_type=MESH
         )
+
+    step = 16
+
+    @pl.loop(0, rows // step)
+    def _(i):
+        at = pl.ds(pl.multiple_of(i * step, step), step)
+        wide = resid_ref[at, :].astype(jnp.float32)
+        scale = lax.rsqrt(jnp.mean(wide * wide, axis=-1, keepdims=True) + 1e-06)
+        gathered[z, q, at, :] = (wide * scale * gain_ref[...]).astype(jnp.bfloat16)
+
+    mix = route_ref[...] / jnp.sum(route_ref[...], axis=0, keepdims=True)
+    for e in range(count):
+        table_ref[e] = jnp.sum(jnp.where(ids_ref[...] == e, mix, 0.0), axis=0, keepdims=True)
+    weights[me] = jnp.sum(jnp.where(ids_ref[...] == me, mix, 0.0), axis=0, keepdims=True)
     pl.semaphore_wait(barrier, count - 1)
 
     started = []
@@ -72,6 +87,17 @@
         return z + jnp.where(k <= 2 * near, paired, -side * (k - near))
 
     plane_of = [visit(k) for k in range(planes)]
+    is_near = [False, True, near >= 1] + [False] * planes
+
+    def when(condition, run):
+        if condition is True:
+            run()
+        elif condition is not False:
+            pl.when(condition)(run)
+
+    def negate(condition):
+        return not condition if isinstance(condition, bool) else jnp.logical_not(condition)
+
     to_y, to_core, to_fwd = {}, {}, {}
     red_core, red_y, red_z = {}, {}, {}
     guarded = []
@@ -85,8 +111,7 @@
 
     def spread(s):
         p = plane_of[s]
-        src = x_ref if s == 0 else gathered.at[p, q]
-        dst = gathered.at[p, q]
+        src = dst = gathered.at[p, q]
         to_y[s] = begin(remote(src, dst, y_send.at[s], y_recv.at[s], y_mate))
         to_core[s] = begin(remote(src, dst, core_send.at[s], core_recv.at[s], core_mate))
 
@@ -101,8 +126,8 @@
         )
 
     spread(0)
-    begin_if(z > 0, z_copy(z, x_ref, 0, jnp.maximum(z - 1, 0)))
-    begin_if(z < planes - 1, z_copy(z, x_ref, planes, jnp.minimum(z + 1, planes - 1)))
+    begin_if(z > 0, z_copy(z, gathered.at[z, q], 0, jnp.maximum(z - 1, 0)))
+    begin_if(z < planes - 1, z_copy(z, gathered.at[z, q], planes, jnp.minimum(z + 1, planes - 1)))
     tables = []
     for k in range(1, count):
         target = lax.rem(me + k, count)
@@ -114,8 +139,17 @@
                 )
             )
         )
-    gathered[z, q] = x_ref[...]
-    weights[me] = table_ref[me]
+    for slot, there in ((0, z > 0), (1, z < planes - 1)):
+
+        @pl.when(jnp.logical_not(there))
+        def _(slot=slot):
+            from_near[slot] = jnp.zeros(from_near.shape[1:], jnp.bfloat16)
+
+    if planes > 2:
+
+        @pl.when(is_near[2])
+        def _():
+            from_z[plane_of[2]] = jnp.zeros(from_z.shape[1:], jnp.bfloat16)
 
     def arrive(s):
         if s >= planes:
@@ -177,10 +211,31 @@
             )
         )
 
-    step = 16
+    def y_copy(s):
+        return remote(
+            partial.at[s, c, flip(y, 1)], from_y.at[s], ry_send.at[s], ry_recv.at[s], y_mate
+        )
+
+    def far_copy(s, source):
+        return remote(
+            partial.at[s, c, y], from_z.at[source], rz_send.at[s], rz_recv.at[source],
+            plane_of[s] * PLANE + q,
+        )
+
+    def near_copy(s, slot):
+        return remote(
+            partial.at[s, c], from_near.at[slot], rn_send.at[s], rn_recv.at[slot],
+            plane_of[s] * PLANE + q,
+        )
 
     def reduce_y(s):
         red_core[s].wait_recv()
+        if s == 0:
+            for slot, there in ((0, z > 0), (1, z < planes - 1)):
+
+                @pl.when(there)
+                def _(slot=slot):
+                    near_copy(0, slot).wait_recv()
 
         @pl.loop(0, rows // step)
         def _(i):
@@ -189,32 +244,29 @@
                 total = partial[s, c, k, at, :].astype(jnp.float32) + from_core[
                     s, k, at, :
                 ].astype(jnp.float32)
+                if s == 0:
+                    for slot in range(2):
+                        total = total + from_near[slot, k, at, :].astype(jnp.float32)
                 partial[s, c, k, at, :] = total.astype(jnp.bfloat16)
 
-        red_y[s] = begin(
-            remote(
-                partial.at[s, c, flip(y, 1)], from_y.at[s], ry_send.at[s], ry_recv.at[s], y_mate
-            )
-        )
+        when(is_near[s], lambda: near_copy(s, jnp.where(plane_of[s] > z, 0, 1)).start())
+        when(negate(is_near[s]), lambda: y_copy(s).start())
 
     def reduce_z(s):
-        red_y[s].wait_recv()
-
-        @pl.loop(0, rows // step)
-        def _(i):
-            at = pl.ds(pl.multiple_of(i * step, step), step)
-            total = partial[s, c, y, at, :].astype(jnp.float32) + from_y[s, at, :].astype(
-                jnp.float32
-            )
-            partial[s, c, y, at, :] = total.astype(jnp.bfloat16)
-
-        if s:
-            red_z[s] = begin(
-                remote(
-                    partial.at[s, c, y], from_z.at[z], rz_send.at[s], rz_recv.at[z],
-                    plane_of[s] * PLANE + q,
+        def run():
+            y_copy(s).wait_recv()
+
+            @pl.loop(0, rows // step)
+            def _(i):
+                at = pl.ds(pl.multiple_of(i * step, step), step)
+                total = partial[s, c, y, at, :].astype(jnp.float32) + from_y[s, at, :].astype(
+                    jnp.float32
                 )
-            )
+                partial[s, c, y, at, :] = total.astype(jnp.bfloat16)
+
+            far_copy(s, z).start()
+
+        when(negate(is_near[s]), run)
 
     arrive(1)
     forward(0)
@@ -234,20 +286,18 @@
             reduce_y(s)
         if s > 1:
             reduce_z(s - 1)
+    if planes > 2:
+        reduce_z(planes - 1)
     reduce_y(0)
-    reduce_z(planes - 1)
-    reduce_z(0)
+    y_copy(0).wait_recv()
     for s in range(1, planes):
-        p = plane_of[s]
-        remote(
-            partial.at[0, c, y], from_z.at[p], rz_send.at[s], rz_recv.at[p], p * PLANE + q
-        ).wait_recv()
+        when(negate(is_near[s]), lambda s=s: far_copy(s, plane_of[s]).wait_recv())
 
     @pl.loop(0, rows // step)
     def _(i):
         at = pl.ds(pl.multiple_of(i * step, step), step)
-        total = partial[0, c, y, at, :].astype(jnp.float32)
-        for s in range(1, planes):
+        total = partial[0, c, y, at, :].astype(jnp.float32) + from_y[0, at, :].astype(jnp.float32)
+        for s in range(2, planes):
             total = total + from_z[plane_of[s], at, :].astype(jnp.float32)
         o_ref[at, :] = (resid_ref[at, :].astype(jnp.float32) + total).astype(jnp.bfloat16)
 
@@ -258,6 +308,16 @@
         @pl.when(condition)
         def _(copy=copy):
             copy.wait_send()
+
+    y_copy(0).wait_send()
+    for s in range(1, planes):
+        when(is_near[s], lambda s=s: near_copy(s, 0).wait_send())
+
+        def sent(s=s):
+            y_copy(s).wait_send()
+            far_copy(s, z).wait_send()
+
+        when(negate(is_near[s]), sent)
 
 
 def vmem_bytes(count, rows, width, units):
@@ -276,13 +336,6 @@
     fits = vmem_bytes(count, rows, width, units) <= 44 * 2**20
     if count % PLANE or planes < 2 or planes & (planes - 1) or rows != 128 or not fits:
         return local_wide(resid, norm_gain, expert_ids, route_weights, w_in, w_out)
-    resid_wide = resid.astype(jnp.float32)
-    scale = lax.rsqrt(jnp.mean(resid_wide * resid_wide, axis=-1, keepdims=True) + 1e-06)
-    normed = (resid_wide * scale * norm_gain).astype(jnp.bfloat16)
-    mix_weights = route_weights / jnp.sum(route_weights, axis=-1, keepdims=True)
-    experts = jnp.arange(count, dtype=jnp.int32)[:, None, None]
-    table = jnp.sum(jnp.where(expert_ids[None] == experts, mix_weights[None], 0.0), axis=-1)
-    table = table.reshape(count, 1, rows)
     vmem = pl.BlockSpec(memory_space=pltpu.VMEM)
     hbm = pl.BlockSpec(memory_space=pl.ANY)
     bf16 = jnp.bfloat16
@@ -290,10 +343,11 @@
     return pl.pallas_call(
         functools.partial(moe_kernel, count),
         out_shape=jax.ShapeDtypeStruct((rows, width), bf16),
-        in_specs=[vmem, vmem, vmem, hbm, hbm],
+        in_specs=[vmem, vmem, vmem, vmem, hbm, hbm],
         out_specs=vmem,
         scratch_shapes=[
             pltpu.VMEM((planes, PLANE, rows, width), bf16),
+            pltpu.VMEM((count, 1, rows), jnp.float32),
             pltpu.VMEM((count, 1, rows), jnp.float32),
             pltpu.VMEM((PLANE * rows, 128), jnp.float32),
             pltpu.VMEM((width, 2 * units), bf16),
@@ -303,15 +357,16 @@
             pltpu.VMEM((planes, 2, rows, width), bf16),
             pltpu.VMEM((planes, rows, width), bf16),
             pltpu.VMEM((planes, rows, width), bf16),
+            pltpu.VMEM((2, 2, rows, width), bf16),
             dma((2,)),
             dma((count - 1,)),
             dma((count - 1,)),
         ]
-        + [dma((planes + 1,))] * 14,
+        + [dma((planes + 1,))] * 16,
         compiler_params=pltpu.CompilerParams(
             collective_id=0, has_side_effects=True, vmem_limit_bytes=60 * 2**20
         ),
-    )(normed, table, resid, w_in, w_out)
+    )(resid, norm_gain[None], expert_ids.T, route_weights.T, w_in, w_out)
 
 
 def local_wide(resid, norm_gain, expert_ids, route_weights, w_in, w_out):

time: 134 us -> 117 us (0.87)
  Pallas kernels: 126 us -> 115 us
  other arithmetic: 5.96 us -> 0 us
    pallas_call x1, Pallas kernels: 126 us -> 115 us  [local(): pl.pallas_call(functools.partial(moe_kernel, count), out_shape=jax.ShapeD...]
    reduce_sum x3 -> x0, other arithmetic: 3.23 us -> none  [the longest x1 1.3 us: local(): jnp.sum(jnp.where(expert_ids[None] == experts, mix_weights[None], 0.0), a...]
    convert_element_type x1 -> x0, other arithmetic: 2.02 us -> none  [local(): normed = (resid_wide * scale * norm_gain).astype(jnp.bfloat16)]
where the time goes in v3:
time: 117 us
  Pallas kernels  115 us (98%)
  local copies, waits for them, and re-layouts  1.88 us (2%)
    pallas_call x1, Pallas kernels, local(): pl.pallas_call(functools.partial(moe_kernel, count), out_shape=jax.ShapeD...  115 us

profile of v3, /device:TPU:0, one launch (start us, length us, event | category | flops | bytes accessed | tf_op | source)
XLA Modules:
  0.0 117.2 jit_solution(7040423641457010519)
XLA Ops:
  0.0 115.3 %shard_map.64 = bf16[128,2048]{1,0:T(8,128)(2,1)} custom-call(bf16[128,2048]{1,0:T(8,128)(2,1)} %resid_ref.1, f32[1,2048]{1,0:T(1,128)} %bitcast.3, s32[8,128]{1,0:T(8,128)} %bitcast.4, f32[8,128]{1,0:T(8,128)} %bitcast.5, bf16[1,2048,1536]{2,1,0:T(8,128)(2,1)} %win_hbm.1, bf16[1,768,2048]{2,1,0:T(8,128)(2,1)} %wout_hbm.1), custom_call_target="tpu_custom_call" | custom-call | tf_op jit(solution)/shard_map/pallas_call | solution.py:343
  115.4 1.9 %copy.8 = bf16[128,2048]{1,0:T(8,128)(2,1)} copy(bf16[128,2048]{1,0:T(8,128)(2,1)} %shard_map.64) | data formatting | bytes 1048576

commit v4 on v3

--- a/solution.py
+++ b/solution.py
@@ -9,6 +9,8 @@
 
 
 PLANE = 4
+PARTS = 2
+LAG = 2
 MESH = pl.DeviceIdType.MESH
 
 
@@ -31,6 +33,7 @@
     rows, width = resid_ref.shape
     units = wout.shape[0]
     planes = count // PLANE
+    part = rows // PARTS
     me = lax.axis_index("ep")
     z, q = me // PLANE, me % PLANE
     y, c = q // 2, q % 2
@@ -56,12 +59,16 @@
 
     step = 16
 
-    @pl.loop(0, rows // step)
-    def _(i):
-        at = pl.ds(pl.multiple_of(i * step, step), step)
-        wide = resid_ref[at, :].astype(jnp.float32)
-        scale = lax.rsqrt(jnp.mean(wide * wide, axis=-1, keepdims=True) + 1e-06)
-        gathered[z, q, at, :] = (wide * scale * gain_ref[...]).astype(jnp.bfloat16)
+    for h in range(PARTS):
+
+        @pl.loop(0, part // step)
+        def _(i, h=h):
+            at = pl.ds(pl.multiple_of(i * step, step), step)
+            wide = resid_ref[pl.ds(pl.multiple_of(h * part + i * step, step), step), :].astype(
+                jnp.float32
+            )
+            scale = lax.rsqrt(jnp.mean(wide * wide, axis=-1, keepdims=True) + 1e-06)
+            gathered[z * PARTS + h, q, at, :] = (wide * scale * gain_ref[...]).astype(jnp.bfloat16)
 
     mix = route_ref[...] / jnp.sum(route_ref[...], axis=0, keepdims=True)
     for e in range(count):
@@ -87,7 +94,10 @@
         return z + jnp.where(k <= 2 * near, paired, -side * (k - near))
 
     plane_of = [visit(k) for k in range(planes)]
-    is_near = [False, True, near >= 1] + [False] * planes
+    near_planes = [False, True, near >= 1] + [False] * planes
+    units_all = planes * PARTS
+    is_near = [near_planes[s // PARTS] for s in range(units_all)]
+    piece_of = [plane_of[s // PARTS] * PARTS + s % PARTS for s in range(units_all)]
 
     def when(condition, run):
         if condition is True:
@@ -110,14 +120,13 @@
         guarded.append((condition, copy))
 
     def spread(s):
-        p = plane_of[s]
-        src = dst = gathered.at[p, q]
+        src = dst = gathered.at[piece_of[s], q]
         to_y[s] = begin(remote(src, dst, y_send.at[s], y_recv.at[s], y_mate))
         to_core[s] = begin(remote(src, dst, core_send.at[s], core_recv.at[s], core_mate))
 
     def forward(s):
         to_y[s].wait_recv()
-        block = gathered.at[plane_of[s], flip(q, 2)]
+        block = gathered.at[piece_of[s], flip(q, 2)]
         to_fwd[s] = begin(remote(block, block, fwd_send.at[s], fwd_recv.at[s], core_mate))
 
     def z_copy(p, src, send, target_plane):
@@ -125,9 +134,14 @@
             src, gathered.at[p, q], z_send.at[send], z_recv.at[p], target_plane * PLANE + q
         )
 
-    spread(0)
-    begin_if(z > 0, z_copy(z, gathered.at[z, q], 0, jnp.maximum(z - 1, 0)))
-    begin_if(z < planes - 1, z_copy(z, gathered.at[z, q], planes, jnp.minimum(z + 1, planes - 1)))
+    for s in range(PARTS):
+        p = piece_of[s]
+        spread(s)
+        begin_if(z > 0, z_copy(p, gathered.at[p, q], s, jnp.maximum(z - 1, 0)))
+        begin_if(
+            z < planes - 1,
+            z_copy(p, gathered.at[p, q], units_all + s, jnp.minimum(z + 1, planes - 1)),
+        )
     tables = []
     for k in range(1, count):
         target = lax.rem(me + k, count)
@@ -143,21 +157,23 @@
 
         @pl.when(jnp.logical_not(there))
         def _(slot=slot):
-            from_near[slot] = jnp.zeros(from_near.shape[1:], jnp.bfloat16)
+            for h in range(PARTS):
+                from_near[slot * PARTS + h] = jnp.zeros(from_near.shape[1:], jnp.bfloat16)
 
     if planes > 2:
 
-        @pl.when(is_near[2])
+        @pl.when(near_planes[2])
         def _():
-            from_z[plane_of[2]] = jnp.zeros(from_z.shape[1:], jnp.bfloat16)
+            for h in range(PARTS):
+                from_z[plane_of[2] * PARTS + h] = jnp.zeros(from_z.shape[1:], jnp.bfloat16)
 
     def arrive(s):
-        if s >= planes:
+        if s >= units_all:
             return
-        p = plane_of[s]
+        p, plane = piece_of[s], plane_of[s // PARTS]
         block = gathered.at[p, q]
-        z_copy(p, block, s, p).wait_recv()
-        onward = jnp.where(p < z, z + 1, z - 1)
+        z_copy(p, block, s, plane).wait_recv()
+        onward = jnp.where(plane < z, z + 1, z - 1)
         inside = jnp.logical_and(onward >= 0, onward < planes)
         begin_if(inside, z_copy(p, block, s, jnp.clip(onward, 0, planes - 1)))
         spread(s)
@@ -166,20 +182,22 @@
     tile_out = 512 if width % 512 == 0 else width
 
     def experts(s):
-        plane = plane_of[s]
+        plane, h = plane_of[s // PARTS], s % PARTS
         eye = lax.broadcasted_iota(jnp.int32, (rows, rows), 0) == lax.broadcasted_iota(
             jnp.int32, (rows, rows), 1
         )
         for k in range(PLANE):
             lane = jnp.broadcast_to(weights[plane * PLANE + k], (rows, rows))
             column = jnp.sum(jnp.where(eye, lane, 0.0), axis=1, keepdims=True)
-            weight_cols[pl.ds(k * rows, rows), :] = jnp.broadcast_to(column, (rows, 128))
+            weight_cols[pl.ds(k * part, part), :] = jnp.broadcast_to(
+                column[h * part : (h + 1) * part], (part, 128)
+            )
 
         @pl.loop(0, units // tile_in)
         def _(j):
             gate_at = pl.multiple_of(j * tile_in, 128)
             up_at = pl.multiple_of(units + j * tile_in, 128)
-            block = gathered[plane].reshape(PLANE * rows, width)
+            block = gathered[piece_of[s]].reshape(PLANE * part, width)
             gate = jnp.dot(
                 block, win[:, pl.ds(gate_at, tile_in)], preferred_element_type=jnp.float32
             )
@@ -195,9 +213,9 @@
             )
             made = made.astype(jnp.bfloat16).astype(jnp.float32)
             for k in range(PLANE):
-                cols = weight_cols[pl.ds(k * rows, rows), :]
+                cols = weight_cols[pl.ds(k * part, part), :]
                 pieces = [
-                    made[k * rows : (k + 1) * rows, i * 128 : (i + 1) * 128] * cols
+                    made[k * part : (k + 1) * part, i * 128 : (i + 1) * 128] * cols
                     for i in range(tile_out // 128)
                 ]
                 partial[s, k % 2, k // 2, :, pl.ds(at, tile_out)] = jnp.concatenate(
@@ -219,44 +237,45 @@
     def far_copy(s, source):
         return remote(
             partial.at[s, c, y], from_z.at[source], rz_send.at[s], rz_recv.at[source],
-            plane_of[s] * PLANE + q,
+            plane_of[s // PARTS] * PLANE + q,
         )
 
     def near_copy(s, slot):
         return remote(
             partial.at[s, c], from_near.at[slot], rn_send.at[s], rn_recv.at[slot],
-            plane_of[s] * PLANE + q,
+            plane_of[s // PARTS] * PLANE + q,
         )
 
     def reduce_y(s):
         red_core[s].wait_recv()
-        if s == 0:
+        if s < PARTS:
             for slot, there in ((0, z > 0), (1, z < planes - 1)):
 
                 @pl.when(there)
                 def _(slot=slot):
-                    near_copy(0, slot).wait_recv()
-
-        @pl.loop(0, rows // step)
+                    near_copy(s, slot * PARTS + s).wait_recv()
+
+        @pl.loop(0, part // step)
         def _(i):
             at = pl.ds(pl.multiple_of(i * step, step), step)
             for k in range(2):
                 total = partial[s, c, k, at, :].astype(jnp.float32) + from_core[
                     s, k, at, :
                 ].astype(jnp.float32)
-                if s == 0:
+                if s < PARTS:
                     for slot in range(2):
-                        total = total + from_near[slot, k, at, :].astype(jnp.float32)
+                        total = total + from_near[slot * PARTS + s, k, at, :].astype(jnp.float32)
                 partial[s, c, k, at, :] = total.astype(jnp.bfloat16)
 
-        when(is_near[s], lambda: near_copy(s, jnp.where(plane_of[s] > z, 0, 1)).start())
+        side_slot = jnp.where(plane_of[s // PARTS] > z, 0, PARTS)
+        when(is_near[s], lambda: near_copy(s, side_slot + s % PARTS).start())
         when(negate(is_near[s]), lambda: y_copy(s).start())
 
     def reduce_z(s):
         def run():
             y_copy(s).wait_recv()
 
-            @pl.loop(0, rows // step)
+            @pl.loop(0, part // step)
             def _(i):
                 at = pl.ds(pl.multiple_of(i * step, step), step)
                 total = partial[s, c, y, at, :].astype(jnp.float32) + from_y[s, at, :].astype(
@@ -264,42 +283,51 @@
                 )
                 partial[s, c, y, at, :] = total.astype(jnp.bfloat16)
 
-            far_copy(s, z).start()
+            far_copy(s, z * PARTS + s % PARTS).start()
 
         when(negate(is_near[s]), run)
 
-    arrive(1)
+    arrive(PARTS)
     forward(0)
     load_in.wait()
     load_out.wait()
     for copy in tables:
         copy.wait_recv()
-    for s in range(planes):
+    arrive(PARTS + 1)
+    for s in range(units_all):
         to_core[s].wait_recv()
         to_fwd[s].wait_recv()
         experts(s)
         reduce_core(s)
-        arrive(s + 2)
-        if s + 1 < planes:
+        arrive(s + PARTS + 2)
+        if s + 1 < units_all:
             forward(s + 1)
-        if s:
+        if s >= PARTS:
             reduce_y(s)
-        if s > 1:
-            reduce_z(s - 1)
-    if planes > 2:
-        reduce_z(planes - 1)
-    reduce_y(0)
-    y_copy(0).wait_recv()
-    for s in range(1, planes):
-        when(negate(is_near[s]), lambda s=s: far_copy(s, plane_of[s]).wait_recv())
-
-    @pl.loop(0, rows // step)
-    def _(i):
-        at = pl.ds(pl.multiple_of(i * step, step), step)
-        total = partial[0, c, y, at, :].astype(jnp.float32) + from_y[0, at, :].astype(jnp.float32)
-        for s in range(2, planes):
-            total = total + from_z[plane_of[s], at, :].astype(jnp.float32)
-        o_ref[at, :] = (resid_ref[at, :].astype(jnp.float32) + total).astype(jnp.bfloat16)
+        if s >= 2 * PARTS + LAG:
+            reduce_z(s - LAG)
+    for s in range(max(units_all - LAG, 2 * PARTS), units_all):
+        reduce_z(s)
+    for s in range(PARTS):
+        reduce_y(s)
+    for s in range(PARTS):
+        y_copy(s).wait_recv()
+    for s in range(2 * PARTS, units_all):
+        when(negate(is_near[s]), lambda s=s: far_copy(s, piece_of[s]).wait_recv())
+
+    for h in range(PARTS):
+
+        @pl.loop(0, part // step)
+        def _(i, h=h):
+            at = pl.ds(pl.multiple_of(i * step, step), step)
+            out_at = pl.ds(pl.multiple_of(h * part + i * step, step), step)
+            total = partial[h, c, y, at, :].astype(jnp.float32)
+            total = total + from_y[h, at, :].astype(jnp.float32)
+            for s in range(2, planes):
+                total = total + from_z[plane_of[s] * PARTS + h, at, :].astype(jnp.float32)
+            o_ref[out_at, :] = (resid_ref[out_at, :].astype(jnp.float32) + total).astype(
+                jnp.bfloat16
+            )
 
     for copy in started:
         copy.wait_send()
@@ -309,13 +337,14 @@
         def _(copy=copy):
             copy.wait_send()
 
-    y_copy(0).wait_send()
-    for s in range(1, planes):
+    for s in range(PARTS):
+        y_copy(s).wait_send()
+    for s in range(PARTS, units_all):
         when(is_near[s], lambda s=s: near_copy(s, 0).wait_send())
 
         def sent(s=s):
             y_copy(s).wait_send()
-            far_copy(s, z).wait_send()
+            far_copy(s, z * PARTS + s % PARTS).wait_send()
 
         when(negate(is_near[s]), sent)
 
@@ -336,6 +365,7 @@
     fits = vmem_bytes(count, rows, width, units) <= 44 * 2**20
     if count % PLANE or planes < 2 or planes & (planes - 1) or rows != 128 or not fits:
         return local_wide(resid, norm_gain, expert_ids, route_weights, w_in, w_out)
+    part, pieces = rows // PARTS, planes * PARTS
     vmem = pl.BlockSpec(memory_space=pltpu.VMEM)
     hbm = pl.BlockSpec(memory_space=pl.ANY)
     bf16 = jnp.bfloat16
@@ -346,23 +376,23 @@
         in_specs=[vmem, vmem, vmem, vmem, hbm, hbm],
         out_specs=vmem,
         scratch_shapes=[
-            pltpu.VMEM((planes, PLANE, rows, width), bf16),
+            pltpu.VMEM((pieces, PLANE, part, width), bf16),
             pltpu.VMEM((count, 1, rows), jnp.float32),
             pltpu.VMEM((count, 1, rows), jnp.float32),
-            pltpu.VMEM((PLANE * rows, 128), jnp.float32),
+            pltpu.VMEM((PLANE * part, 128), jnp.float32),
             pltpu.VMEM((width, 2 * units), bf16),
             pltpu.VMEM((units, width), bf16),
-            pltpu.VMEM((PLANE * rows, units), bf16),
-            pltpu.VMEM((planes, 2, 2, rows, width), bf16),
-            pltpu.VMEM((planes, 2, rows, width), bf16),
-            pltpu.VMEM((planes, rows, width), bf16),
-            pltpu.VMEM((planes, rows, width), bf16),
-            pltpu.VMEM((2, 2, rows, width), bf16),
+            pltpu.VMEM((PLANE * part, units), bf16),
+            pltpu.VMEM((pieces, 2, 2, part, width), bf16),
+            pltpu.VMEM((pieces, 2, part, width), bf16),
+            pltpu.VMEM((pieces, part, width), bf16),
+            pltpu.VMEM((pieces, part, width), bf16),
+            pltpu.VMEM((2 * PARTS, 2, part, width), bf16),
             dma((2,)),
             dma((count - 1,)),
             dma((count - 1,)),
         ]
-        + [dma((planes + 1,))] * 16,
+        + [dma((pieces + PARTS,))] * 16,
         compiler_params=pltpu.CompilerParams(
             collective_id=0, has_side_effects=True, vmem_limit_bytes=60 * 2**20
         ),

time: 117 us -> 115 us (0.983)
  Pallas kernels: 115 us -> 113 us
    pallas_call x1, Pallas kernels: 115 us -> 113 us  [local(): pl.pallas_call(functools.partial(moe_kernel, count), out_shape=jax.ShapeD...]
where the time goes in v4:
time: 115 us
  Pallas kernels  113 us (98%)
  local copies, waits for them, and re-layouts  1.88 us (2%)
    pallas_call x1, Pallas kernels, local(): pl.pallas_call(functools.partial(moe_kernel, count), out_shape=jax.ShapeD...  113 us

profile of v4, /device:TPU:0, one launch (start us, length us, event | category | flops | bytes accessed | tf_op | source)
XLA Modules:
  0.0 115.2 jit_solution(8213789723659941498)
XLA Ops:
  0.0 113.3 %shard_map.64 = bf16[128,2048]{1,0:T(8,128)(2,1)} custom-call(bf16[128,2048]{1,0:T(8,128)(2,1)} %resid_ref.1, f32[1,2048]{1,0:T(1,128)} %bitcast.3, s32[8,128]{1,0:T(8,128)} %bitcast.4, f32[8,128]{1,0:T(8,128)} %bitcast.5, bf16[1,2048,1536]{2,1,0:T(8,128)(2,1)} %win_hbm.1, bf16[1,768,2048]{2,1,0:T(8,128)(2,1)} %wout_hbm.1), custom_call_target="tpu_custom_call" | custom-call | tf_op jit(solution)/shard_map/pallas_call | solution.py:373
  113.3 1.9 %copy.8 = bf16[128,2048]{1,0:T(8,128)(2,1)} copy(bf16[128,2048]{1,0:T(8,128)(2,1)} %shard_map.64) | data formatting | bytes 1048576
